TPU v7x, 128 devices: a whole 4x4x4 slice. The times are simulated.
128 devices in a mesh: cfg: 2 (over core), seq: 64 (over z, y, x).
Axes of the slice: x: 4, y: 4, z: 4, core: 2. Of those that a mesh axis runs over, the one named last changes fastest.
Arguments:
- hidden: bfloat16 [2, 512, 3072], P('cfg', 'seq'), may hold values from -6 to 6
- latent: float32 [512, 64], P('seq', 'cfg'), may hold values from -6 to 6
- positions: int32 [512, 3], P('seq'), may hold values from 0 to 44
- counts: int32 [64], replicated, may hold values from 4 to 8
- text_len: int32 [1], replicated, may hold values from 1 to 255
- modulation: float32 [2, 6, 3072], replicated, may hold values from -3 to 3
- w_qkv: bfloat16 [3072, 3, 3072], P(None, None, 'seq'), may hold values from -0.109375 to 0.109375
- w_out: bfloat16 [3072, 3072], P('seq'), may hold values from -0.109375 to 0.109375
- w_up: bfloat16 [3072, 12288], P(None, 'seq'), may hold values from -0.109375 to 0.109375
- w_down: bfloat16 [12288, 3072], P('seq'), may hold values from -0.0546875 to 0.0546875
- out_mod: float32 [2, 3072], replicated, may hold values from -3 to 3
- w_proj: bfloat16 [3072, 64], replicated, may hold values from -0.109375 to 0.109375
- guidance: float32 [1], replicated, may hold values from 3 to 8
- solver: float32 [2], replicated, may hold values from 0.3 to 1
Outputs:
- next_latent: float32 [512, 64], P('seq', 'cfg')
All inputs are finite; a program needn't handle non-finite values.
Results may differ from a plain program's by a relative error of at most 0.009.
Values may be sent and summed in bfloat16 or wider, within the bound.
A program may use at most 128 MiB of HBM per device.

v0:
```python
import jax
import jax.numpy as jnp
from jax import lax
from jax.sharding import PartitionSpec as P

D = 3072
HD = 64


def partner_2(block, axis, bit):
    count = lax.axis_size(axis)
    route = []
    for low in range(count):
        high = low | 1 << bit
        if high != low and high < count:
            route += [(low, high), (high, low)]
    return lax.ppermute(block, axis, route)


def layer_norm(values, epsilon):
    center = values - jnp.mean(values, axis=-1, keepdims=True)
    spread = jnp.mean(center * center, axis=-1, keepdims=True)
    return center * lax.rsqrt(spread + epsilon)


def rotary_angles(position_rows, head_size):
    places = position_rows.astype(jnp.float32)
    frame_pairs = head_size // 8
    side_pairs = 3 * head_size // 16
    frame_freq = 10000.0 ** (-2.0 * jnp.arange(frame_pairs, dtype=jnp.float32) / (head_size // 4))
    side_freq = 10000.0 ** (-2.0 * jnp.arange(side_pairs, dtype=jnp.float32) / (3 * head_size // 8))
    return jnp.concatenate(
        [
            places[:, 0:1] * frame_freq[None, :],
            places[:, 1:2] * side_freq[None, :],
            places[:, 2:3] * side_freq[None, :],
        ],
        axis=1,
    )


def prepare_heads(columns, cosine, sine, heads, head_size):
    values = columns.astype(jnp.float32).reshape(columns.shape[0], heads, head_size)
    values = layer_norm(values, 1e-06)
    pairs = values.reshape(columns.shape[0], heads, head_size // 2, 2)
    first = pairs[..., 0]
    second = pairs[..., 1]
    cos_rows = cosine[:, None, :]
    sin_rows = sine[:, None, :]
    turned = jnp.stack(
        [first * cos_rows - second * sin_rows, first * sin_rows + second * cos_rows], axis=-1
    )
    return turned.reshape(columns.shape[0], heads * head_size).astype(jnp.bfloat16)


def shards(
    hidden,
    latent,
    positions,
    counts,
    text_len,
    modulation,
    w_qkv,
    w_out,
    w_up,
    w_down,
    out_mod,
    w_proj,
    guidance,
    solver,
):
    heads = D // HD
    resid = hidden[0].astype(jnp.float32)
    rows = resid.shape[0]
    groups = lax.axis_size("seq")
    total = rows * groups
    myself = lax.axis_index("seq")
    slot_all = jnp.arange(total)
    live_all = jnp.where(slot_all % rows < jnp.repeat(counts, rows), 1.0, 0.0).astype(jnp.float32)
    own_slots = myself * rows + jnp.arange(rows)
    live_own = jnp.arange(rows) < counts[myself]
    is_text = own_slots < text_len[0]
    angles = rotary_angles(positions, HD) * jnp.where(is_text, 0.0, 1.0)[:, None].astype(
        jnp.float32
    )
    cosine = jnp.cos(angles)
    sine = jnp.sin(angles)

    def modul(index):
        return jnp.where(
            is_text[:, None], modulation[0, index][None, :], modulation[1, index][None, :]
        )

    normed = (layer_norm(resid, 1e-05) * (1.0 + modul(1)) + modul(0)).astype(jnp.bfloat16)
    width_cols = w_qkv.shape[2]
    qkv_weight = w_qkv.reshape(D, 3 * width_cols)
    qkv_cols = jnp.dot(
        lax.all_gather(normed, "seq", axis=0, tiled=True),
        qkv_weight,
        preferred_element_type=jnp.float32,
    ).astype(jnp.bfloat16)
    qkv_cols = qkv_cols.reshape(total, 3, width_cols)
    qkv = lax.all_to_all(qkv_cols, "seq", split_axis=0, concat_axis=2, tiled=True)
    queries = prepare_heads(qkv[:, 0], cosine, sine, heads, HD)
    keys_rot = prepare_heads(qkv[:, 1], cosine, sine, heads, HD)
    values = qkv[:, 2]
    q_three = queries.reshape(rows, heads, HD)
    key_piece = lax.all_gather(keys_rot, "seq", axis=0, tiled=True)
    value_piece = lax.all_gather(values, "seq", axis=0, tiled=True)
    count = key_piece.shape[0]
    scores = jnp.einsum(
        "qhd,khd->hqk",
        q_three,
        key_piece.reshape(count, heads, HD),
        preferred_element_type=jnp.float32,
    ) * HD ** (-0.5)
    weights = jnp.exp(scores) * live_all[None, None, :]
    denom = jnp.sum(weights, axis=2).T
    numer = jnp.einsum(
        "hqk,khd->qhd",
        weights.astype(jnp.bfloat16),
        value_piece.reshape(count, heads, HD),
        preferred_element_type=jnp.float32,
    )
    numer, denom = (numer, denom)
    context = (numer / denom[:, :, None]).reshape(rows, D).astype(jnp.bfloat16)
    attended = jnp.dot(
        context,
        lax.all_gather(w_out, "seq", axis=0, tiled=True),
        preferred_element_type=jnp.float32,
    )
    first_res = resid + modul(2) * attended
    normed_two = (layer_norm(first_res, 1e-05) * (1.0 + modul(4)) + modul(3)).astype(jnp.bfloat16)
    inner_all = jax.nn.gelu(
        jnp.dot(
            lax.all_gather(normed_two, "seq", axis=0, tiled=True),
            w_up,
            preferred_element_type=jnp.float32,
        ),
        approximate=True,
    ).astype(jnp.bfloat16)
    reduced = lax.psum_scatter(
        jnp.dot(inner_all, w_down, preferred_element_type=jnp.float32),
        "seq",
        scatter_dimension=0,
        tiled=True,
    )
    second_res = first_res + modul(5) * reduced
    final = (
        layer_norm(second_res, 1e-05) * (1.0 + out_mod[1][None, :]) + out_mod[0][None, :]
    ).astype(jnp.bfloat16)
    prediction = jnp.dot(final, w_proj, preferred_element_type=jnp.float32)
    half_cols = latent.shape[1]
    branch_side = lax.axis_index("cfg")
    own_pred = lax.dynamic_slice_in_dim(prediction, branch_side * half_cols, half_cols, 1)
    other_cols = lax.dynamic_slice_in_dim(prediction, (1 - branch_side) * half_cols, half_cols, 1)
    partner = partner_2(other_cols, "cfg", 0)
    is_cond = branch_side == 0
    pred_cond = jnp.where(is_cond, own_pred, partner)
    pred_uncond = jnp.where(is_cond, partner, own_pred)
    guided = pred_uncond + guidance[0] * (pred_cond - pred_uncond)
    updated = solver[0] * latent + solver[1] * guided
    return jnp.where((live_own & jnp.logical_not(is_text))[:, None], updated, latent)


def solution(mesh):
    in_specs = (
        P("cfg", "seq", None),
        P("seq", "cfg"),
        P("seq", None),
        P(),
        P(),
        P(),
        P(None, None, "seq"),
        P("seq", None),
        P(None, "seq"),
        P("seq", None),
        P(),
        P(),
        P(),
        P(),
    )
    out_specs = P("seq", "cfg")
    return jax.shard_map(shards, mesh=mesh, in_specs=in_specs, out_specs=out_specs, check_vma=False)
```

profile of v0, /device:TPU:1, one launch (start us, length us, event | category | flops | bytes accessed | tf_op | source)
XLA Modules:
  0.0 701.4 jit_solution(6040464034356221136)
XLA Ops:
  7.3 1.7 fusion.43
  10.9 1.2 dynamic_slice.9
  12.2 1.2 not_and_fusion
  13.4 1.5 fusion.26
  15.8 68.7 %all-gather.7.cloned.1.call-done = bf16[512,3072]{1,0:T(8,128)(2,1)} async-done(((bf16[8,3072]{1,0:T(8,128)(2,1)}), bf16[512,3072]{1,0:T(8,128)(2,1)}) %all-gather.7.cloned.1.call-update) | async-done | bytes 3145744 | tf_op jit(solution)/shard_map/all_gather | solution.py:98
  84.5 3.3 convolution_convert_fusion
  88.2 1.2 reshape.258
  89.4 6.1 all-to-all-start
  96.5 8.0 %all-to-all-done = bf16[64,2,576]{2,1,0:T(2,128)(2,1)S(1)} async-done(((bf16[64,2,576]{2,1,0:T(2,128)(2,1)}), bf16[64,2,576]{2,1,0:T(2,128)(2,1)S(1)}, u32[]{:S(2)}, u32[]{:S(2)}) %all-to-all-start) | async-done | bytes 147488 | tf_op jit(solution)/shard_map/all_to_all | solution.py:103
  107.9 1.7 copy.70
  109.7 3.9 subtract_multiply_fusion
  113.6 6.4 slice_multiply_fusion.5
  120.0 3.3 copy.73
  123.3 3.3 copy.74
  126.7 3.3 copy.75
  130.0 3.3 copy.76
  136.0 3.4 copy.77
  139.3 2.0 copy.78
  144.4 3.3 copy.65
  147.8 1.7 copy.66
  151.9 54.2 %all-gather.9.cloned.1.call-done = bf16[512,3072]{1,0:T(8,128)(2,1)} async-done(((bf16[8,3072]{1,0:T(8,128)(2,1)}), bf16[512,3072]{1,0:T(8,128)(2,1)}) %all-gather.9.cloned.1.call-update) | async-done | bytes 3145744 | tf_op jit(solution)/shard_map/all_gather | solution.py:108
  206.1 4.7 copy.79
  210.8 62.7 %all-gather.15.cloned.1.call-done = bf16[512,1,3072]{2,0,1:T(8,128)(2,1)} async-done(((bf16[8,1,3072]{2,0,1:T(8,128)(2,1)}), bf16[512,1,3072]{2,0,1:T(8,128)(2,1)}) %all-gather.15.cloned.1.call-update) | async-done | bytes 3145744 | tf_op jit(solution)/shard_map/all_gather | solution.py:109
  273.6 4.7 copy.59
  278.3 2.7 fusion.45
  282.2 102.8 %all-gather.11.cloned.1.call-done = bf16[3072,3072]{1,0:T(8,128)(2,1)} async-done(((bf16[48,3072]{1,0:T(8,128)(2,1)}), bf16[3072,3072]{1,0:T(8,128)(2,1)}) %all-gather.11.cloned.1.call-update) | async-done | bytes 18874384 | tf_op jit(solution)/shard_map/all_gather | solution.py:129
  385.1 7.9 %fusion.46 = (f32[8]{0:T(128)S(1)}, f32[8,3072]{1,0:T(8,128)S(1)}) fusion(bf16[8,3072]{1,0:T(8,128)(2,1)S(1)} %convert_element_type.101, bf16[3072,3072]{1,0:T(8,128)(2,1)} %all-gather.11.cloned.1.call-done, f32[3072]{0:T(1024)S(1)} %bitcast.93, f32[3072]{0:T(1024)S(1)} %bitcast.94, pred[8]{0:T(512)(128)(4,1)S(1)} %copy-done.16, ...), kind=kOutput, calls=%fused_computation.105 | convolution fusion | flops 151117824 | bytes 19095592 | tf_op jit(solution)/shard_map/dot_general | solution.py:127
  394.1 65.9 %all-gather.13.cloned.1.call-done = bf16[512,3072]{1,0:T(8,128)(2,1)} async-done(((bf16[8,3072]{1,0:T(8,128)(2,1)}), bf16[512,3072]{1,0:T(8,128)(2,1)}) %all-gather.13.cloned.1.call-update) | async-done | bytes 3145744 | tf_op jit(solution)/shard_map/all_gather | solution.py:136
  460.0 6.8 fusion.14
  467.6 219.5 %reduce-scatter.2.cloned.1.call-done = f32[8,3072]{1,0:T(8,128)} async-done(((f32[512,3072]{1,0:T(8,128)}), f32[8,3072]{1,0:T(8,128)}) %reduce-scatter.2.cloned.1.call-update) | async-done | bytes 98320 | tf_op jit(solution)/shard_map/reduce_scatter | solution.py:142
  688.7 2.6 collective-permute-start
  692.7 1.9 add_select_fusion
  (119 shorter events, 21.0 us)
Async XLA Ops:
  6.5 453.5 %copy-start = (bf16[192,3072]{1,0:T(8,128)(2,1)S(1)}, bf16[192,3072]{1,0:T(8,128)(2,1)}, u32[]{:S(2)}) copy-start(bf16[192,3072]{1,0:T(8,128)(2,1)} %param.23) | copy-start | bytes 3538948
  6.5 78.0 %all-gather.7.cloned.1.call-start = ((), (), s32[]{:S(2)}) async-start(), calls=%async_computation.2 | async-start | bytes 3194880 | tf_op jit(solution)/shard_map/all_gather | solution.py:98
  13.4 74.4 %copy-start.15 = (pred[8]{0:T(512)(128)(4,1)}, pred[8]{0:T(512)(128)(4,1)S(1)}, u32[]{:S(2)}) copy-start(pred[8]{0:T(512)(128)(4,1)S(1)} %get-tuple-element.6) | copy-start | bytes 28
  89.4 15.1 %all-to-all-start = ((bf16[64,2,576]{2,1,0:T(2,128)(2,1)}), bf16[64,2,576]{2,1,0:T(2,128)(2,1)S(1)}, u32[]{:S(2)}, u32[]{:S(2)}) async-start(bf16[64,2,576]{2,1,0:T(2,128)(2,1)} %reshape.258), calls=%async_computation | async-start | bytes 327680 | tf_op jit(solution)/shard_map/all_to_all | solution.py:103
  95.5 110.6 %all-gather.9.cloned.1.call-start = ((), (), s32[]{:S(2)}) async-start(), calls=%async_computation.3 | async-start | bytes 3194880 | tf_op jit(solution)/shard_map/all_gather | solution.py:108
  109.7 3.9 copy-start.5
  123.3 19.6 %copy-start.20 = (s32[64]{0:T(128)S(1)}, s32[64]{0:T(128)}, u32[]{:S(2)}) copy-start(s32[64]{0:T(128)} %param.17) | copy-start | bytes 772
  141.4 132.2 %all-gather.15.cloned.1.call-start = ((), (), s32[]{:S(2)}) async-start(), calls=%async_computation.7 | async-start | bytes 3194880 | tf_op jit(solution)/shard_map/all_gather | solution.py:109
  142.1 243.0 %all-gather.11.cloned.1.call-start = ((), (), s32[]{:S(2)}) async-start(), calls=%async_computation.4 | async-start | bytes 19169280 | tf_op jit(solution)/shard_map/all_gather | solution.py:129
  142.7 317.3 %all-gather.13.cloned.1.call-start = ((), (), s32[]{:S(2)}) async-start(), calls=%async_computation.5 | async-start | bytes 3194880 | tf_op jit(solution)/shard_map/all_gather | solution.py:136
  278.3 2.8 copy-start.1
  278.3 106.8 %copy-start.3 = (bf16[1,8,3072]{2,1,0:T(8,128)(2,1)S(1)}, bf16[1,8,3072]{2,1,0:T(8,128)(2,1)}, u32[]{:S(2)}) copy-start(bf16[1,8,3072]{2,1,0:T(8,128)(2,1)} %param.14) | copy-start | bytes 147460
  278.3 106.8 %copy-start.6 = (f32[1,1,3072]{2,0,1:T(1,128)S(1)}, f32[1,1,3072]{2,0,1:T(1,128)}, u32[]{:S(2)}) copy-start(f32[1,1,3072]{2,0,1:T(1,128)} %get-tuple-element.31) | copy-start | bytes 36868
  278.3 106.8 %copy-start.7 = (f32[1,1,3072]{2,0,1:T(1,128)S(1)}, f32[1,1,3072]{2,0,1:T(1,128)}, u32[]{:S(2)}) copy-start(f32[1,1,3072]{2,0,1:T(1,128)} %get-tuple-element.32) | copy-start | bytes 36868
  278.3 106.8 %copy-start.16 = (pred[8]{0:T(512)(128)(4,1)S(1)}, pred[8]{0:T(512)(128)(4,1)}, u32[]{:S(2)}) copy-start(pred[8]{0:T(512)(128)(4,1)} %copy-done.15) | copy-start | bytes 28
  385.1 8.2 %copy-start.10 = (f32[1,1,3072]{2,0,1:T(1,128)S(1)}, f32[1,1,3072]{2,0,1:T(1,128)}, u32[]{:S(2)}) copy-start(f32[1,1,3072]{2,0,1:T(1,128)} %get-tuple-element.24) | copy-start | bytes 36868
  385.1 8.2 %copy-start.11 = (f32[1,1,3072]{2,0,1:T(1,128)S(1)}, f32[1,1,3072]{2,0,1:T(1,128)}, u32[]{:S(2)}) copy-start(f32[1,1,3072]{2,0,1:T(1,128)} %get-tuple-element.25) | copy-start | bytes 36868
  385.1 8.2 %copy-start.12 = (f32[1,1,3072]{2,0,1:T(1,128)S(1)}, f32[1,1,3072]{2,0,1:T(1,128)}, u32[]{:S(2)}) copy-start(f32[1,1,3072]{2,0,1:T(1,128)} %get-tuple-element.33) | copy-start | bytes 36868
  385.1 8.2 %copy-start.13 = (f32[1,1,3072]{2,0,1:T(1,128)S(1)}, f32[1,1,3072]{2,0,1:T(1,128)}, u32[]{:S(2)}) copy-start(f32[1,1,3072]{2,0,1:T(1,128)} %get-tuple-element.34) | copy-start | bytes 36868
  385.1 74.9 %copy-start.2 = (bf16[3072,192]{0,1:T(8,128)(2,1)S(1)}, bf16[3072,192]{0,1:T(8,128)(2,1)}, u32[]{:S(2)}) copy-start(bf16[3072,192]{0,1:T(8,128)(2,1)} %param.22) | copy-start | bytes 3538948
  394.0 293.0 %reduce-scatter.2.cloned.1.call-start = ((), (), s32[]{:S(2)}) async-start(), calls=%async_computation.6 | async-start | bytes 6389760 | tf_op jit(solution)/shard_map/reduce_scatter | solution.py:142
  466.8 0.7 copy-start.14
  466.8 220.3 %copy-start.8 = (f32[1,1,3072]{2,0,1:T(1,128)S(1)}, f32[1,1,3072]{2,0,1:T(1,128)}, u32[]{:S(2)}) copy-start(f32[1,1,3072]{2,0,1:T(1,128)} %get-tuple-element.23) | copy-start | bytes 36868
  466.8 220.3 %copy-start.9 = (f32[1,1,3072]{2,0,1:T(1,128)S(1)}, f32[1,1,3072]{2,0,1:T(1,128)}, u32[]{:S(2)}) copy-start(f32[1,1,3072]{2,0,1:T(1,128)} %get-tuple-element.26) | copy-start | bytes 36868
  466.8 221.6 %copy-start.4 = (bf16[3072,64]{0,1:T(8,128)(2,1)S(1)}, bf16[3072,64]{0,1:T(8,128)(2,1)}, u32[]{:S(2)}) copy-start(bf16[3072,64]{0,1:T(8,128)(2,1)} %param.25) | copy-start | bytes 1179652
  466.8 224.6 %copy-start.19 = (f32[2]{0:T(128)S(1)}, f32[2]{0:T(128)}, u32[]{:S(2)}) copy-start(f32[2]{0:T(128)} %param.27) | copy-start | bytes 28
  466.8 225.8 %copy-start.17 = (f32[8,32]{1,0:T(8,128)S(1)}, f32[8,32]{1,0:T(8,128)}, u32[]{:S(2)}) copy-start(f32[8,32]{1,0:T(8,128)} %param.15) | copy-start | bytes 3076
  466.8 225.8 %copy-start.18 = (pred[8]{0:T(512)(128)(4,1)S(1)}, pred[8]{0:T(512)(128)(4,1)}, u32[]{:S(2)}) copy-start(pred[8]{0:T(512)(128)(4,1)} %get-tuple-element.5) | copy-start | bytes 28
  688.7 3.9 collective-permute-start
Sparse Core Ops, SparseCore 0:
  15.1 69.4 all-gather.6
  141.5 64.5 all-gather.8
  208.9 64.6 all-gather.14
  276.2 108.8 all-gather.10
  394.2 65.7 all-gather.12
  467.0 220.0 reduce-scatter.1
where the time goes:
time: 703 us; the launch traced here: 701 us
  waiting for transfers between devices  583 us (83%)
  local copies, waits for them, and re-layouts  46.8 us (7%)
  other arithmetic  25.2 us (4%)
  matrix products  21.8 us (3%)
  between operations  15.3 us (2%)
  starting transfers between devices  9.13 us (1%)
    reduce_scatter x1, waiting for transfers between devices, shards(): lax.psum_scatter(jnp.dot(inner_all, w_down, preferred_element_type=jnp.fl...  219 us
    all_gather x1, waiting for transfers between devices, shards(): lax.all_gather(w_out, 'seq', axis=0, tiled=True)  103 us
    all_gather x1, waiting for transfers between devices, shards(): lax.all_gather(normed, 'seq', axis=0, tiled=True)  68.7 us
    all_gather x1, waiting for transfers between devices, shards(): lax.all_gather(normed_two, 'seq', axis=0, tiled=True)  65.9 us
    all_gather x1, waiting for transfers between devices, shards(): value_piece = lax.all_gather(values, 'seq', axis=0, tiled=True)  62.7 us
    all_gather x1, waiting for transfers between devices, shards(): key_piece = lax.all_gather(keys_rot, 'seq', axis=0, tiled=True)  54.2 us
  transfers between devices with their start and end apart: 8, of which 7 were waited for; matrix products, arithmetic and copies ran while one was open for 3% of the time, Pallas kernels for 0%

commit v1 on v0

v1 whole, which is shorter than its diff:
```python
import functools

import jax
import jax.numpy as jnp
import numpy as np
from jax import lax
from jax.experimental import pallas as pl
from jax.experimental.pallas import tpu as pltpu
from jax.sharding import PartitionSpec as P

D = 3072
HD = 64
SIDE = 4
ROWS = 8
HALF = D // 2
HC = 192
HID = 192
PAD = 128
BF = jnp.bfloat16
F32 = jnp.float32
NT = (((1,), (1,)), ((), ()))


def layer_norm(values, epsilon):
    center = values - jnp.mean(values, axis=-1, keepdims=True)
    spread = jnp.mean(center * center, axis=-1, keepdims=True)
    return center * lax.rsqrt(spread + epsilon)


def dot_nt(a, b):
    return lax.dot_general(a, b, NT, preferred_element_type=F32)


def exact_dot(a, b):
    return lax.dot_general(
        a,
        b,
        (((1,), (0,)), ((), ())),
        preferred_element_type=F32,
        precision=lax.Precision.HIGHEST,
    )


def frequencies():
    frame = 10000.0 ** (-2.0 * np.arange(8) / 16)
    side = 10000.0 ** (-2.0 * np.arange(12) / 24)
    pairs = np.concatenate([frame, side, side])
    return np.tile(np.repeat(pairs, 2), 3)[None, :].astype(np.float32)


def kernel(
    hidden,
    latent,
    pos,
    counts_row,
    counts,
    text_len,
    modulation,
    freq,
    w_qkv,
    w_out,
    w_up,
    w_down,
    out_mod,
    w_proj,
    guidance,
    solver,
    out,
    wqkv,
    wout,
    wup,
    wdown,
    ag1a,
    ag1b,
    ag2a,
    ag2b,
    rows32,
    kv,
    rs1,
    rs2,
    swap,
    w_send,
    w_recv,
    f_send,
    f_recv,
    local_sem,
    c_send,
    c_recv,
):
    cfg = lax.axis_index("cfg")
    me = lax.axis_index("seq")
    z, y, x = me // 16, (me // 4) % 4, me % 4

    def dev(axis, step):
        zz = (z + step) % 4 if axis == "z" else z
        yy = (y + step) % 4 if axis == "y" else y
        xx = (x + step) % 4 if axis == "x" else x
        return (cfg, zz * 16 + yy * 4 + xx)

    place = {"x": x, "y": y, "z": z}
    sibling = (1 - cfg, me)
    sends = []

    def remote(src, dst, send, recv, device):
        copy = pltpu.make_async_remote_copy(
            src_ref=src,
            dst_ref=dst,
            send_sem=send,
            recv_sem=recv,
            device_id=device,
            device_id_type=pl.DeviceIdType.MESH,
        )
        copy.start()
        sends.append(copy)
        return copy

    barrier = pltpu.get_barrier_semaphore()
    everyone = [dev(axis, step) for axis in "xyz" for step in (1, 2, 3)] + [sibling]
    for device in everyone:
        pl.semaphore_signal(
            barrier, inc=1, device_id=device, device_id_type=pl.DeviceIdType.MESH
        )

    mine = pl.ds(pl.multiple_of(cfg * HALF, HALF), HALF)

    weights = {
        "qkv": (0, w_qkv, lambda i: wqkv.at[:, i], "x"),
        "out": (1, w_out, lambda i: wout.at[i], "x"),
        "up": (2, w_up, lambda i: wup.at[i], "y"),
        "down": (3, w_down, lambda i: wdown.at[i], "y"),
    }

    def half_of(ref):
        return ref.at[:, :, mine] if len(ref.shape) == 3 else ref.at[:, mine]

    pending = {}

    def start_weight(name):
        slot, src, dst, axis = weights[name]
        pending[name] = [
            remote(
                half_of(src),
                half_of(dst(place[axis])),
                w_send.at[slot, step - 1],
                w_recv.at[slot, step - 1],
                dev(axis, step),
            )
            for step in (1, 3, 2)
        ]

    def forward_weight(name):
        slot, src, dst, axis = weights[name]
        passed = []
        for step, copy in zip((1, 3, 2), pending[name]):
            copy.wait_recv()
            block = half_of(dst((place[axis] - step + 4) % 4))
            passed.append(
                remote(
                    block,
                    block,
                    f_send.at[slot, step - 1],
                    f_recv.at[slot, step - 1],
                    sibling,
                )
            )
        pending[name] = passed

    def finish_weight(name):
        slot = weights[name][0]
        for copy in pending[name]:
            copy.wait_recv()
        local[slot].wait()

    local = []
    for slot, src, dst, axis in weights.values():
        copy = pltpu.make_async_copy(src, dst(place[axis]), local_sem.at[slot])
        copy.start()
        local.append(copy)

    resid = hidden[...].astype(F32)
    row = lax.broadcasted_iota(jnp.int32, (ROWS, 1), 0)
    is_text = me * ROWS + row < text_len[0]

    def modul(k):
        two = modulation[k]
        return jnp.where(is_text, two[0:1, :], two[1:2, :])

    normed = (layer_norm(resid, 1e-05) * (1.0 + modul(1)) + modul(0)).astype(BF)

    def gather_start(bufs, values, p, q):
        for buf, value, (one, two) in zip(bufs, values, ((p, q), (q, p))):
            for i, part in enumerate(value):
                lo = 0 if i == 0 else HALF
                buf[place[two], place[one], :, lo : lo + part.shape[1]] = part

    def gather_send(bufs, p, q, slot, phase):
        copies = []
        for h, (buf, (one, two)) in enumerate(zip(bufs, ((p, q), (q, p)))):
            for step in (1, 3, 2):
                ref = (
                    buf.at[place[two], place[one]] if phase == 0 else buf.at[place[two]]
                )
                copies.append(
                    remote(
                        ref,
                        ref,
                        c_send.at[slot, phase, h, step - 1],
                        c_recv.at[slot, phase, h, step - 1],
                        dev(one if phase == 0 else two, step),
                    )
                )
        return copies

    def gather_to_rows(bufs):
        for q_at in range(SIDE):
            for p_at in range(SIDE):
                at = (q_at * SIDE + p_at) * ROWS
                rows32[at : at + ROWS, 0:HALF] = bufs[0][q_at, p_at, :, 0:HALF].astype(F32)
                rows32[at : at + ROWS, HALF:D] = bufs[1][p_at, q_at, :, 0:HALF].astype(F32)

    gather_start(
        (ag1a, ag1b), ((normed[:, 0:HALF], pos[...]), (normed[:, HALF:D],)), "y", "z"
    )

    pl.semaphore_wait(barrier, len(everyone))

    first = gather_send((ag1a, ag1b), "y", "z", 0, 0)
    start_weight("qkv")
    for copy in first:
        copy.wait_recv()
    second = gather_send((ag1a, ag1b), "y", "z", 0, 1)

    lane_a = lax.broadcasted_iota(jnp.int32, (HC, HC), 0)
    lane_b = lax.broadcasted_iota(jnp.int32, (HC, HC), 1)
    average = jnp.where(lane_a // HD == lane_b // HD, 1.0 / HD, 0.0).astype(F32)
    turn = (
        jnp.where((lane_a == lane_b + 1) & (lane_b % 2 == 0), -1.0, 0.0)
        + jnp.where((lane_a + 1 == lane_b) & (lane_b % 2 == 1), 1.0, 0.0)
    ).astype(F32)
    key = lax.broadcasted_iota(jnp.int32, (64, 512), 1)
    owner = (key // 32) % 4 * 16 + (key // 8) % 4 * 4 + key // 128
    pick = jnp.where(lax.broadcasted_iota(jnp.int32, (64, 512), 0) == owner, 1.0, 0.0)
    count_of = exact_dot(
        jnp.broadcast_to(counts_row[...].astype(F32), (ROWS, 64)), pick.astype(F32)
    )
    key_row = lax.broadcasted_iota(jnp.int32, (ROWS, 512), 1) % ROWS
    live = jnp.where(key_row.astype(F32) < count_of, 1.0, 0.0)[0:1, :]
    dim = lax.broadcasted_iota(jnp.int32, (PAD, HC), 1) % HD
    which = jnp.where(dim < 16, 0, jnp.where(dim < 40, 1, 2))
    axis_of = jnp.where(
        lax.broadcasted_iota(jnp.int32, (PAD, HC), 0) == which, 1.0, 0.0
    ).astype(F32)

    for copy in second:
        copy.wait_recv()
    start_weight("out")
    start_weight("up")
    start_weight("down")
    gather_to_rows((ag1a, ag1b))
    for z_at in range(SIDE):
        for y_at in range(SIDE):
            at = (z_at * SIDE + y_at) * ROWS
            swap[at : at + ROWS, :] = ag1a[z_at, y_at, :, HALF : HALF + PAD].astype(F32)
    angles = exact_dot(swap[...], axis_of) * freq[...]
    cosine = jnp.cos(angles)
    sine = jnp.sin(angles)
    tokens = rows32[...].astype(BF)

    forward_weight("qkv")
    finish_weight("qkv")

    def heads(columns):
        values = columns.astype(BF).astype(F32)
        center = values - exact_dot(values, average)
        spread = exact_dot(center * center, average)
        unit = center * lax.rsqrt(spread + 1e-06)
        return unit * cosine + exact_dot(unit, turn) * sine

    def project(part):
        return dot_nt(tokens, wqkv[part].reshape(HC, D))

    keys = heads(project(1)).astype(BF)
    kv[x, :, 0:HC] = keys
    kv[x, :, HC : 2 * HC] = project(2).astype(BF)
    moved = [
        remote(
            kv.at[x],
            kv.at[x],
            c_send.at[4, 0, 0, step - 1],
            c_recv.at[4, 0, 0, step - 1],
            dev("x", step),
        )
        for step in (1, 3, 2)
    ]
    queries = (heads(project(0)) * HD ** (-0.5)).astype(BF)
    for copy in moved:
        copy.wait_recv()
    forward_weight("out")

    all_keys = kv[:, :, 0:HC].reshape(4 * 128, HC)
    all_values = kv[:, :, 128 : 2 * HC].reshape(4 * 128, 2 * HC - 128)
    lane_q = lax.broadcasted_iota(jnp.int32, (1, HC), 1) // HD
    lane_v = lax.broadcasted_iota(jnp.int32, (1, 256), 1) // HD - 1
    context = jnp.zeros((128, 256), F32)
    for head in range(HC // HD):
        chosen = jnp.where(lane_q == head, queries, jnp.zeros_like(queries))
        attend = jnp.exp(dot_nt(chosen, all_keys)) * live
        denom = jnp.sum(attend, axis=1, keepdims=True)
        numer = jnp.dot(attend.astype(BF), all_values, preferred_element_type=F32)
        context = jnp.where(lane_v == head, numer / denom, context)
    context = context[:, 64:256].astype(BF)
    finish_weight("out")

    def scatter_sum(send, recv, mid, last, produce, p, q, slot):
        order = ((q, p), (p, q))
        copies = [[], []]
        for h in range(2):
            part = produce(h)
            for q_at in range(SIDE):
                for p_at in range(SIDE):
                    at = (q_at * SIDE + p_at) * ROWS
                    i, j = (q_at, p_at) if h == 0 else (p_at, q_at)
                    send[h, i, j] = part[at : at + ROWS, :].astype(BF)
            for step in (1, 3, 2):
                one = order[h][0]
                copies[h].append(
                    remote(
                        send.at[h, (place[one] + step) % 4],
                        recv.at[h, step - 1],
                        c_send.at[slot, 0, h, step - 1],
                        c_recv.at[slot, 0, h, step - 1],
                        dev(one, step),
                    )
                )
        second = [[], []]
        for h in range(2):
            one, two = order[h]
            for copy in copies[h]:
                copy.wait_recv()
            for j in range(SIDE):
                total = send[h, place[one], j].astype(F32)
                for k in range(3):
                    total = total + recv[h, k, j].astype(F32)
                mid[h, j] = total.astype(BF)
            for step in (1, 3, 2):
                second[h].append(
                    remote(
                        mid.at[h, (place[two] + step) % 4],
                        last.at[h, step - 1],
                        c_send.at[slot, 1, h, step - 1],
                        c_recv.at[slot, 1, h, step - 1],
                        dev(two, step),
                    )
                )
        halves = []
        for h in range(2):
            one, two = order[h]
            for copy in second[h]:
                copy.wait_recv()
            total = mid[h, place[two]].astype(F32)
            for k in range(3):
                total = total + last[h, k].astype(F32)
            halves.append(total)
        return jnp.concatenate(halves, axis=1)

    out_weight = wout[...].reshape(HC, D)
    attended = scatter_sum(
        *rs1,
        lambda h: jnp.dot(
            context, out_weight[:, h * HALF : (h + 1) * HALF], preferred_element_type=F32
        ),
        "y",
        "z",
        1,
    )
    first_res = resid + modul(2) * attended
    normed_two = (layer_norm(first_res, 1e-05) * (1.0 + modul(4)) + modul(3)).astype(BF)
    gather_start(
        (ag2a, ag2b), ((normed_two[:, 0:HALF],), (normed_two[:, HALF:D],)), "x", "z"
    )
    for copy in gather_send((ag2a, ag2b), "x", "z", 2, 0):
        copy.wait_recv()
    second = gather_send((ag2a, ag2b), "x", "z", 2, 1)
    forward_weight("up")
    for copy in second:
        copy.wait_recv()
    gather_to_rows((ag2a, ag2b))
    tokens_two = rows32[...].astype(BF)
    finish_weight("up")
    inner = jax.nn.gelu(
        dot_nt(tokens_two, wup[...].reshape(SIDE * HID, D)), approximate=True
    ).astype(BF)
    forward_weight("down")
    finish_weight("down")
    down_weight = wdown[...].reshape(SIDE * HID, D)
    reduced = scatter_sum(
        *rs2,
        lambda h: jnp.dot(
            inner, down_weight[:, h * HALF : (h + 1) * HALF], preferred_element_type=F32
        ),
        "x",
        "z",
        3,
    )
    second_res = first_res + modul(5) * reduced
    final = (
        layer_norm(second_res, 1e-05) * (1.0 + out_mod[1:2, :]) + out_mod[0:1, :]
    ).astype(BF)
    prediction = dot_nt(final, w_proj[...])
    swap[0:ROWS, 0:64] = prediction
    other = remote(
        swap.at[0:ROWS], swap.at[ROWS : 2 * ROWS], c_send.at[4, 1, 0, 0], c_recv.at[4, 1, 0, 0], sibling
    )
    other.wait_recv()
    theirs = swap[ROWS : 2 * ROWS, 0:64]
    is_cond = cfg == 0
    pred_cond = jnp.where(is_cond, prediction, theirs)
    pred_uncond = jnp.where(is_cond, theirs, prediction)
    guided = pred_uncond + guidance[0] * (pred_cond - pred_uncond)
    guided = jnp.where(is_cond, guided[:, 0:32], guided[:, 32:64])
    updated = solver[0] * latent[...] + solver[1] * guided
    keep = (row < counts[me]) & jnp.logical_not(is_text)
    out[...] = jnp.where(keep, updated, latent[...])
    for copy in sends:
        copy.wait_send()


def shards(
    hidden,
    latent,
    positions,
    counts,
    text_len,
    modulation,
    w_qkv,
    w_out,
    w_up,
    w_down,
    out_mod,
    w_proj,
    guidance,
    solver,
):
    slots = lax.axis_index("seq") * ROWS + jnp.arange(ROWS)
    places = jnp.where((slots < text_len[0])[:, None], 0, positions).astype(BF)
    pos = jnp.pad(places, ((0, 0), (0, PAD - 3)))
    vmem = pl.BlockSpec(memory_space=pltpu.VMEM)
    smem = pl.BlockSpec(memory_space=pltpu.SMEM)
    whole = pl.BlockSpec(memory_space=pl.ANY)

    def sums():
        return (
            pltpu.VMEM((2, SIDE, SIDE, ROWS, HALF), BF),
            pltpu.VMEM((2, 3, SIDE, ROWS, HALF), BF),
            pltpu.VMEM((2, SIDE, ROWS, HALF), BF),
            pltpu.VMEM((2, 3, ROWS, HALF), BF),
        )

    return pl.pallas_call(
        kernel,
        out_shape=jax.ShapeDtypeStruct(latent.shape, F32),
        in_specs=[vmem, vmem, vmem, vmem, smem, smem, vmem, vmem]
        + [whole] * 4
        + [vmem, vmem, smem, smem],
        out_specs=vmem,
        scratch_shapes=[
            pltpu.VMEM((3, SIDE, 48, D), BF),
            pltpu.VMEM((SIDE, 48, D), BF),
            pltpu.VMEM((SIDE, HID, D), BF),
            pltpu.VMEM((SIDE, HID, D), BF),
            pltpu.VMEM((SIDE, SIDE, ROWS, HALF + PAD), BF),
            pltpu.VMEM((SIDE, SIDE, ROWS, HALF), BF),
            pltpu.VMEM((SIDE, SIDE, ROWS, HALF), BF),
            pltpu.VMEM((SIDE, SIDE, ROWS, HALF), BF),
            pltpu.VMEM((SIDE * SIDE * ROWS, D), F32),
            pltpu.VMEM((SIDE, SIDE * SIDE * ROWS, 2 * HC), BF),
            sums(),
            sums(),
            pltpu.VMEM((SIDE * SIDE * ROWS, PAD), F32),
            pltpu.SemaphoreType.DMA((4, 3)),
            pltpu.SemaphoreType.DMA((4, 3)),
            pltpu.SemaphoreType.DMA((4, 3)),
            pltpu.SemaphoreType.DMA((4, 3)),
            pltpu.SemaphoreType.DMA((4,)),
            pltpu.SemaphoreType.DMA((5, 2, 2, 3)),
            pltpu.SemaphoreType.DMA((5, 2, 2, 3)),
        ],
        compiler_params=pltpu.CompilerParams(
            collective_id=0, has_side_effects=True, vmem_limit_bytes=56 << 20
        ),
        name="step",
    )(
        hidden[0],
        latent,
        pos,
        counts[None, :],
        counts,
        text_len,
        modulation.transpose(1, 0, 2),
        jnp.asarray(frequencies()),
        w_qkv.transpose(1, 2, 0),
        w_out,
        w_up.T,
        w_down,
        out_mod,
        w_proj.T,
        guidance,
        solver,
    )


def solution(mesh):
    in_specs = (
        P("cfg", "seq", None),
        P("seq", "cfg"),
        P("seq", None),
        P(),
        P(),
        P(),
        P(None, None, "seq"),
        P("seq", None),
        P(None, "seq"),
        P("seq", None),
        P(),
        P(),
        P(),
        P(),
    )
    return jax.shard_map(
        shards, mesh=mesh, in_specs=in_specs, out_specs=P("seq", "cfg"), check_vma=False
    )
```

time: 703 us -> 113 us (0.16)
  waiting for transfers between devices: 583 us -> 0 us
  Pallas kernels: 0 us -> 108 us
  local copies, waits for them, and re-layouts: 46.8 us -> 2.62 us
  other arithmetic: 25.2 us -> 0.08 us
  matrix products: 21.8 us -> 0 us
  between operations: 15.3 us -> 1.31 us
  starting transfers between devices: 9.13 us -> 0 us
    all_gather x5 -> x0, waiting for transfers between devices: 354 us -> none  [the longest x1 103 us: shards(): lax.all_gather(w_out, 'seq', axis=0, tiled=True)]
    reduce_scatter x1 -> x0, waiting for transfers between devices: 219 us -> none  [shards(): lax.psum_scatter(jnp.dot(inner_all, w_down, preferred_element_type=jnp.fl...]
    pallas_call x0 -> x1, Pallas kernels: none -> 108 us  [shards(): pl.pallas_call(kernel, out_shape=jax.ShapeDtypeStruct(latent.shape, F32),...]
    dot_general x6 -> x0, matrix products: 21.8 us -> none  [the longest x1 7.92 us: shards(): jnp.dot(context, lax.all_gather(w_out, 'seq', axis=0, tiled=True), prefer...]
    mul x9 -> x0, local copies, waits for them, and re-layouts: 19.5 us -> none  [the longest x2 6.68 us: prepare_heads(): first * cos_rows - second * sin_rows]
    mul x4 -> x0, other arithmetic: 10.4 us -> none  [the longest x1 6.36 us: prepare_heads(): second * sin_rows]
    all_gather x2 -> x0, local copies, waits for them, and re-layouts: 9.46 us -> none  [the longest x1 4.73 us: shards(): value_piece = lax.all_gather(values, 'seq', axis=0, tiled=True)]
    all_to_all x1 -> x0, waiting for transfers between devices: 7.98 us -> none  [shards(): lax.all_to_all(qkv_cols, 'seq', split_axis=0, concat_axis=2, tiled=True)]
  transfers between devices with their start and end apart: 8 -> 0, of which waited for: 7 -> 0; matrix products, arithmetic and copies ran while one was open for 3% -> 0% of each run, Pallas kernels for 0% -> 0%
where the time goes in v1:
time: 113 us; the launch traced here: 112 us
  Pallas kernels  108 us (96%)
  local copies, waits for them, and re-layouts  2.62 us (2%)
  between operations  1.31 us (1%)
    pallas_call x1, Pallas kernels, shards(): pl.pallas_call(kernel, out_shape=jax.ShapeDtypeStruct(latent.shape, F32),...  108 us

profile of v1, /device:TPU:1, one launch (start us, length us, event | category | flops | bytes accessed | tf_op | source)
XLA Modules:
  0.0 112.5 jit_solution(7752889240135100237)
XLA Ops:
  1.3 0.8 copy.16
  2.1 0.1 select_convert_fusion
  2.1 0.6 pad.4.pos
  2.7 108.4 %step.1 = f32[8,32]{1,0:T(8,128)} custom-call(bf16[8,3072]{1,0:T(8,128)(2,1)} %bitcast.12, f32[8,32]{1,0:T(8,128)} %latent.1, bf16[8,128]{1,0:T(8,128)(2,1)} %pad.4.pos, s32[1,64]{1,0:T(1,128)} %bitcast.13, s32[64]{0:T(128)} %counts.1, s32[1]{0:T(128)} %copy.18.text_len, f32[6,2,3072]{2,1,0:T(2,128)} %bitcast.11, f32[1,192]{1,0:T(1,128)} %constant.12.clone.freq, ...), custom_call_target="tpu_custom_call" | custom-call | tf_op jit(solution)/shard_map/step/pallas_call | solution.py:459
  111.2 1.3 %copy.20 = f32[8,32]{1,0:T(8,128)} copy(f32[8,32]{1,0:T(8,128)} %step.1) | data formatting | bytes 2048
  (1 shorter events, 0.0 us)

commit v2 on v1

--- a/solution.py
+++ b/solution.py
@@ -49,23 +49,27 @@
 
 
 def kernel(
-    hidden,
     latent,
-    pos,
     counts_row,
+    freq,
+    positions,
     counts,
     text_len,
-    modulation,
-    freq,
+    guidance,
+    solver,
+    hidden_far,
+    modulation_far,
+    out_mod_far,
+    w_proj_far,
     w_qkv,
     w_out,
     w_up,
     w_down,
+    out,
+    hidden,
+    modulation,
     out_mod,
     w_proj,
-    guidance,
-    solver,
-    out,
     wqkv,
     wout,
     wup,
@@ -81,8 +85,7 @@
     swap,
     w_send,
     w_recv,
-    f_send,
-    f_recv,
+    near_sem,
     local_sem,
     c_send,
     c_recv,
@@ -121,62 +124,97 @@
             barrier, inc=1, device_id=device, device_id_type=pl.DeviceIdType.MESH
         )
 
-    mine = pl.ds(pl.multiple_of(cfg * HALF, HALF), HALF)
+    near = []
+    for i, (far, ref) in enumerate(
+        (
+            (hidden_far, hidden),
+            (modulation_far, modulation),
+            (out_mod_far, out_mod),
+            (w_proj_far, w_proj),
+        )
+    ):
+        copy = pltpu.make_async_copy(far, ref, near_sem.at[i])
+        copy.start()
+        near.append(copy)
 
     weights = {
-        "qkv": (0, w_qkv, lambda i: wqkv.at[:, i], "x"),
-        "out": (1, w_out, lambda i: wout.at[i], "x"),
-        "up": (2, w_up, lambda i: wup.at[i], "y"),
-        "down": (3, w_down, lambda i: wdown.at[i], "y"),
+        "k": (0, w_qkv.at[1], lambda i: wqkv.at[1, i], "x"),
+        "v": (1, w_qkv.at[2], lambda i: wqkv.at[2, i], "x"),
+        "q": (2, w_qkv.at[0], lambda i: wqkv.at[0, i], "x"),
+        "out": (3, w_out, lambda i: wout.at[i], "x"),
+        "up": (4, w_up, lambda i: wup.at[i], "y"),
+        "down": (5, w_down, lambda i: wdown.at[i], "y"),
     }
-
-    def half_of(ref):
-        return ref.at[:, :, mine] if len(ref.shape) == 3 else ref.at[:, mine]
-
-    pending = {}
-
-    def start_weight(name):
+    start = pl.multiple_of(cfg * HALF, HALF)
+    half = pl.ds(start, HALF)
+    quarters = (
+        pl.ds(start, HALF // 2),
+        pl.ds(pl.multiple_of(start + HALF // 2, HALF // 2), HALF // 2),
+    )
+    turns = (1, 3)
+    moving = {}
+    local = []
+
+    def send_weight(name):
         slot, src, dst, axis = weights[name]
-        pending[name] = [
+        moving[name, 0] = [
             remote(
-                half_of(src),
-                half_of(dst(place[axis])),
-                w_send.at[slot, step - 1],
-                w_recv.at[slot, step - 1],
-                dev(axis, step),
+                src.at[:, half],
+                dst(place[axis]).at[:, half],
+                w_send.at[slot, 0, i],
+                w_recv.at[slot, 0, i],
+                dev(axis, turn),
             )
-            for step in (1, 3, 2)
+            for i, turn in enumerate(turns)
         ]
 
-    def forward_weight(name):
+    def pass_weight(name):
         slot, src, dst, axis = weights[name]
-        passed = []
-        for step, copy in zip((1, 3, 2), pending[name]):
-            copy.wait_recv()
-            block = half_of(dst((place[axis] - step + 4) % 4))
-            passed.append(
+        moving[name, 1], moving[name, 2] = [], []
+        for i, turn in enumerate(turns):
+            moving[name, 0][i].wait_recv()
+            block = dst((place[axis] - turn + 4) % 4)
+            moving[name, 1].append(
                 remote(
-                    block,
-                    block,
-                    f_send.at[slot, step - 1],
-                    f_recv.at[slot, step - 1],
+                    block.at[:, quarters[i]],
+                    block.at[:, quarters[i]],
+                    w_send.at[slot, 1, i],
+                    w_recv.at[slot, 1, i],
+                    dev(axis, turn),
+                )
+            )
+            moving[name, 2].append(
+                remote(
+                    block.at[:, half],
+                    block.at[:, half],
+                    w_send.at[slot, 2, i],
+                    w_recv.at[slot, 2, i],
                     sibling,
                 )
             )
-        pending[name] = passed
-
-    def finish_weight(name):
-        slot = weights[name][0]
-        for copy in pending[name]:
+
+    def end_weight(name):
+        slot, src, dst, axis = weights[name]
+        for copy in moving[name, 1]:
             copy.wait_recv()
-        local[slot].wait()
-
-    local = []
-    for slot, src, dst, axis in weights.values():
-        copy = pltpu.make_async_copy(src, dst(place[axis]), local_sem.at[slot])
-        copy.start()
-        local.append(copy)
-
+        block = dst((place[axis] + 2) % 4)
+        moving[name, 2].append(
+            remote(
+                block.at[:, half],
+                block.at[:, half],
+                w_send.at[slot, 3, 0],
+                w_recv.at[slot, 3, 0],
+                sibling,
+            )
+        )
+
+    def have_weight(name):
+        for copy in moving[name, 2]:
+            copy.wait_recv()
+        local[weights[name][0]].wait()
+
+    near[0].wait()
+    near[1].wait()
     resid = hidden[...].astype(F32)
     row = lax.broadcasted_iota(jnp.int32, (ROWS, 1), 0)
     is_text = me * ROWS + row < text_len[0]
@@ -218,17 +256,32 @@
                 rows32[at : at + ROWS, 0:HALF] = bufs[0][q_at, p_at, :, 0:HALF].astype(F32)
                 rows32[at : at + ROWS, HALF:D] = bufs[1][p_at, q_at, :, 0:HALF].astype(F32)
 
+    lane = lax.broadcasted_iota(jnp.int32, (ROWS, PAD), 1)
+    line = lax.broadcasted_iota(jnp.int32, (ROWS, PAD), 0)
+    pos = jnp.zeros((ROWS, PAD), F32)
+    for k in range(3):
+        for r in range(ROWS):
+            at = positions[k, r].astype(F32)
+            pos = jnp.where((lane == k) & (line == r), at, pos)
+    pos = jnp.where(is_text, 0.0, pos).astype(BF)
     gather_start(
-        (ag1a, ag1b), ((normed[:, 0:HALF], pos[...]), (normed[:, HALF:D],)), "y", "z"
+        (ag1a, ag1b), ((normed[:, 0:HALF], pos), (normed[:, HALF:D],)), "y", "z"
     )
 
     pl.semaphore_wait(barrier, len(everyone))
 
     first = gather_send((ag1a, ag1b), "y", "z", 0, 0)
-    start_weight("qkv")
+    for name in ("k", "v", "q", "out"):
+        send_weight(name)
+    for slot, src, dst, axis in weights.values():
+        copy = pltpu.make_async_copy(src, dst(place[axis]), local_sem.at[slot])
+        copy.start()
+        local.append(copy)
     for copy in first:
         copy.wait_recv()
     second = gather_send((ag1a, ag1b), "y", "z", 0, 1)
+    send_weight("up")
+    send_weight("down")
 
     lane_a = lax.broadcasted_iota(jnp.int32, (HC, HC), 0)
     lane_b = lax.broadcasted_iota(jnp.int32, (HC, HC), 1)
@@ -251,11 +304,10 @@
         lax.broadcasted_iota(jnp.int32, (PAD, HC), 0) == which, 1.0, 0.0
     ).astype(F32)
 
+    for name in ("k", "v", "q"):
+        pass_weight(name)
     for copy in second:
         copy.wait_recv()
-    start_weight("out")
-    start_weight("up")
-    start_weight("down")
     gather_to_rows((ag1a, ag1b))
     for z_at in range(SIDE):
         for y_at in range(SIDE):
@@ -266,8 +318,9 @@
     sine = jnp.sin(angles)
     tokens = rows32[...].astype(BF)
 
-    forward_weight("qkv")
-    finish_weight("qkv")
+    pass_weight("out")
+    for name in ("k", "v", "q"):
+        end_weight(name)
 
     def heads(columns):
         values = columns.astype(BF).astype(F32)
@@ -279,7 +332,9 @@
     def project(part):
         return dot_nt(tokens, wqkv[part].reshape(HC, D))
 
+    have_weight("k")
     keys = heads(project(1)).astype(BF)
+    have_weight("v")
     kv[x, :, 0:HC] = keys
     kv[x, :, HC : 2 * HC] = project(2).astype(BF)
     moved = [
@@ -292,10 +347,11 @@
         )
         for step in (1, 3, 2)
     ]
+    have_weight("q")
     queries = (heads(project(0)) * HD ** (-0.5)).astype(BF)
     for copy in moved:
         copy.wait_recv()
-    forward_weight("out")
+    end_weight("out")
 
     all_keys = kv[:, :, 0:HC].reshape(4 * 128, HC)
     all_values = kv[:, :, 128 : 2 * HC].reshape(4 * 128, 2 * HC - 128)
@@ -309,9 +365,9 @@
         numer = jnp.dot(attend.astype(BF), all_values, preferred_element_type=F32)
         context = jnp.where(lane_v == head, numer / denom, context)
     context = context[:, 64:256].astype(BF)
-    finish_weight("out")
-
-    def scatter_sum(send, recv, mid, last, produce, p, q, slot):
+    have_weight("out")
+
+    def scatter_sum(send, recv, mid, last, produce, p, q, slot, meanwhile):
         order = ((q, p), (p, q))
         copies = [[], []]
         for h in range(2):
@@ -332,6 +388,7 @@
                         dev(one, step),
                     )
                 )
+        meanwhile()
         second = [[], []]
         for h in range(2):
             one, two = order[h]
@@ -372,6 +429,7 @@
         "y",
         "z",
         1,
+        lambda: pass_weight("up"),
     )
     first_res = resid + modul(2) * attended
     normed_two = (layer_norm(first_res, 1e-05) * (1.0 + modul(4)) + modul(3)).astype(BF)
@@ -381,17 +439,18 @@
     for copy in gather_send((ag2a, ag2b), "x", "z", 2, 0):
         copy.wait_recv()
     second = gather_send((ag2a, ag2b), "x", "z", 2, 1)
-    forward_weight("up")
+    pass_weight("down")
+    end_weight("up")
     for copy in second:
         copy.wait_recv()
     gather_to_rows((ag2a, ag2b))
     tokens_two = rows32[...].astype(BF)
-    finish_weight("up")
+    end_weight("down")
+    have_weight("up")
     inner = jax.nn.gelu(
         dot_nt(tokens_two, wup[...].reshape(SIDE * HID, D)), approximate=True
     ).astype(BF)
-    forward_weight("down")
-    finish_weight("down")
+    have_weight("down")
     down_weight = wdown[...].reshape(SIDE * HID, D)
     reduced = scatter_sum(
         *rs2,
@@ -401,7 +460,10 @@
         "x",
         "z",
         3,
-    )
+        lambda: None,
+    )
+    near[2].wait()
+    near[3].wait()
     second_res = first_res + modul(5) * reduced
     final = (
         layer_norm(second_res, 1e-05) * (1.0 + out_mod[1:2, :]) + out_mod[0:1, :]
@@ -441,9 +503,6 @@
     guidance,
     solver,
 ):
-    slots = lax.axis_index("seq") * ROWS + jnp.arange(ROWS)
-    places = jnp.where((slots < text_len[0])[:, None], 0, positions).astype(BF)
-    pos = jnp.pad(places, ((0, 0), (0, PAD - 3)))
     vmem = pl.BlockSpec(memory_space=pltpu.VMEM)
     smem = pl.BlockSpec(memory_space=pltpu.SMEM)
     whole = pl.BlockSpec(memory_space=pl.ANY)
@@ -459,11 +518,13 @@
     return pl.pallas_call(
         kernel,
         out_shape=jax.ShapeDtypeStruct(latent.shape, F32),
-        in_specs=[vmem, vmem, vmem, vmem, smem, smem, vmem, vmem]
-        + [whole] * 4
-        + [vmem, vmem, smem, smem],
+        in_specs=[vmem] * 3 + [smem] * 5 + [whole] * 8,
         out_specs=vmem,
         scratch_shapes=[
+            pltpu.VMEM((ROWS, D), BF),
+            pltpu.VMEM((6, 2, D), F32),
+            pltpu.VMEM((2, D), F32),
+            pltpu.VMEM((64, D), BF),
             pltpu.VMEM((3, SIDE, 48, D), BF),
             pltpu.VMEM((SIDE, 48, D), BF),
             pltpu.VMEM((SIDE, HID, D), BF),
@@ -477,11 +538,10 @@
             sums(),
             sums(),
             pltpu.VMEM((SIDE * SIDE * ROWS, PAD), F32),
-            pltpu.SemaphoreType.DMA((4, 3)),
-            pltpu.SemaphoreType.DMA((4, 3)),
-            pltpu.SemaphoreType.DMA((4, 3)),
-            pltpu.SemaphoreType.DMA((4, 3)),
+            pltpu.SemaphoreType.DMA((6, 4, 2)),
+            pltpu.SemaphoreType.DMA((6, 4, 2)),
             pltpu.SemaphoreType.DMA((4,)),
+            pltpu.SemaphoreType.DMA((6,)),
             pltpu.SemaphoreType.DMA((5, 2, 2, 3)),
             pltpu.SemaphoreType.DMA((5, 2, 2, 3)),
         ],
@@ -490,22 +550,22 @@
         ),
         name="step",
     )(
-        hidden[0],
         latent,
-        pos,
         counts[None, :],
+        jnp.asarray(frequencies()),
+        positions.T,
         counts,
         text_len,
+        guidance,
+        solver,
+        hidden[0],
         modulation.transpose(1, 0, 2),
-        jnp.asarray(frequencies()),
+        out_mod,
+        w_proj.T,
         w_qkv.transpose(1, 2, 0),
         w_out,
         w_up.T,
         w_down,
-        out_mod,
-        w_proj.T,
-        guidance,
-        solver,
     )
 
 

time: 113 us -> 86.9 us (0.77)
  Pallas kernels: 108 us -> 84.2 us
  local copies, waits for them, and re-layouts: 2.62 us -> 1.28 us
    pallas_call x1, Pallas kernels: 108 us -> 84.2 us  [shards(): pl.pallas_call(kernel, out_shape=jax.ShapeDtypeStruct(latent.shape, F32),...]
where the time goes in v2:
time: 86.9 us; the launch traced here: 86.7 us
  Pallas kernels  84.2 us (97%)
  between operations  1.3 us (1%)
  local copies, waits for them, and re-layouts  1.28 us (1%)
    pallas_call x1, Pallas kernels, shards(): pl.pallas_call(kernel, out_shape=jax.ShapeDtypeStruct(latent.shape, F32),...  84.2 us

profile of v2, /device:TPU:1, one launch (start us, length us, event | category | flops | bytes accessed | tf_op | source)
XLA Modules:
  0.0 86.7 jit_solution(11936201660788721978)
XLA Ops:
  1.3 84.2 %step.1 = f32[8,32]{1,0:T(8,128)} custom-call(f32[8,32]{1,0:T(8,128)} %latent.1, s32[1,64]{1,0:T(1,128)} %bitcast.13, f32[1,192]{1,0:T(1,128)} %constant.2.clone.freq, s32[3,8]{1,0:T(4,128)} %bitcast.12, s32[64]{0:T(128)} %counts.1, s32[1]{0:T(128)S(6)} %copy.17.text_len, f32[1]{0:T(128)S(6)} %copy.18.guidance, f32[2]{0:T(128)} %solver.1, ...), custom_call_target="tpu_custom_call" | custom-call | tf_op jit(solution)/shard_map/step/pallas_call | solution.py:518
  85.5 1.3 %copy.19 = f32[8,32]{1,0:T(8,128)} copy(f32[8,32]{1,0:T(8,128)} %step.1) | data formatting | bytes 2048

commit v3 on v2

--- a/solution.py
+++ b/solution.py
@@ -89,6 +89,8 @@
     local_sem,
     c_send,
     c_recv,
+    g_send,
+    g_recv,
 ):
     cfg = lax.axis_index("cfg")
     me = lax.axis_index("seq")
@@ -137,13 +139,16 @@
         copy.start()
         near.append(copy)
 
+    top, bottom = pl.ds(0, HID // 2), pl.ds(HID // 2, HID // 2)
     weights = {
         "k": (0, w_qkv.at[1], lambda i: wqkv.at[1, i], "x"),
         "v": (1, w_qkv.at[2], lambda i: wqkv.at[2, i], "x"),
         "q": (2, w_qkv.at[0], lambda i: wqkv.at[0, i], "x"),
         "out": (3, w_out, lambda i: wout.at[i], "x"),
-        "up": (4, w_up, lambda i: wup.at[i], "y"),
-        "down": (5, w_down, lambda i: wdown.at[i], "y"),
+        "up0": (4, w_up.at[top], lambda i: wup.at[i, top], "y"),
+        "up1": (5, w_up.at[bottom], lambda i: wup.at[i, bottom], "y"),
+        "down0": (6, w_down.at[top], lambda i: wdown.at[i, top], "y"),
+        "down1": (7, w_down.at[bottom], lambda i: wdown.at[i, bottom], "y"),
     }
     start = pl.multiple_of(cfg * HALF, HALF)
     half = pl.ds(start, HALF)
@@ -225,36 +230,61 @@
 
     normed = (layer_norm(resid, 1e-05) * (1.0 + modul(1)) + modul(0)).astype(BF)
 
-    def gather_start(bufs, values, p, q):
-        for buf, value, (one, two) in zip(bufs, values, ((p, q), (q, p))):
+    def gather_own(bufs, values, orders):
+        for buf, value, (p, q) in zip(bufs, values, orders):
             for i, part in enumerate(value):
                 lo = 0 if i == 0 else HALF
-                buf[place[two], place[one], :, lo : lo + part.shape[1]] = part
-
-    def gather_send(bufs, p, q, slot, phase):
-        copies = []
-        for h, (buf, (one, two)) in enumerate(zip(bufs, ((p, q), (q, p)))):
-            for step in (1, 3, 2):
-                ref = (
-                    buf.at[place[two], place[one]] if phase == 0 else buf.at[place[two]]
-                )
-                copies.append(
+                buf[place[q], place[p], :, lo : lo + part.shape[1]] = part
+
+    def gather_first(bufs, orders, slot):
+        first = []
+        for h, (buf, (p, q)) in enumerate(zip(bufs, orders)):
+            ref = buf.at[place[q], place[p]]
+            first.append(
+                [
                     remote(
                         ref,
                         ref,
-                        c_send.at[slot, phase, h, step - 1],
-                        c_recv.at[slot, phase, h, step - 1],
-                        dev(one if phase == 0 else two, step),
+                        g_send.at[slot, h, 0, step - 1],
+                        g_recv.at[slot, h, 0, step - 1],
+                        dev(p, step),
                     )
-                )
-        return copies
-
-    def gather_to_rows(bufs):
-        for q_at in range(SIDE):
-            for p_at in range(SIDE):
-                at = (q_at * SIDE + p_at) * ROWS
-                rows32[at : at + ROWS, 0:HALF] = bufs[0][q_at, p_at, :, 0:HALF].astype(F32)
-                rows32[at : at + ROWS, HALF:D] = bufs[1][p_at, q_at, :, 0:HALF].astype(F32)
+                    for step in (1, 3, 2)
+                ]
+            )
+        return first, [gather_pass(bufs[h], orders[h], slot, h, 0) for h in range(2)]
+
+    def gather_pass(buf, order, slot, h, behind):
+        p, q = order
+        ref = buf.at[place[q], (place[p] - behind + 4) % 4]
+        return [
+            remote(
+                ref,
+                ref,
+                g_send.at[slot, h, behind + 1, step - 1],
+                g_recv.at[slot, h, behind + 1, step - 1],
+                dev(q, step),
+            )
+            for step in (1, 3, 2)
+        ]
+
+    def gather_second(bufs, orders, slot, state):
+        first, second = state
+        for i, behind in enumerate((1, 3, 2)):
+            for h in range(2):
+                first[h][i].wait_recv()
+                second[h] += gather_pass(bufs[h], orders[h], slot, h, behind)
+
+    def gather_end(bufs, orders, outer, state):
+        for copy in state[1][0] + state[1][1]:
+            copy.wait_recv()
+        for h, (buf, (p, q)) in enumerate(zip(bufs, orders)):
+            for i in range(SIDE):
+                for j in range(SIDE):
+                    at = (i * SIDE + j if q == outer else j * SIDE + i) * ROWS
+                    rows32[at : at + ROWS, h * HALF : (h + 1) * HALF] = buf[
+                        i, j, :, 0:HALF
+                    ].astype(F32)
 
     lane = lax.broadcasted_iota(jnp.int32, (ROWS, PAD), 1)
     line = lax.broadcasted_iota(jnp.int32, (ROWS, PAD), 0)
@@ -264,24 +294,26 @@
             at = positions[k, r].astype(F32)
             pos = jnp.where((lane == k) & (line == r), at, pos)
     pos = jnp.where(is_text, 0.0, pos).astype(BF)
-    gather_start(
-        (ag1a, ag1b), ((normed[:, 0:HALF], pos), (normed[:, HALF:D],)), "y", "z"
+    order_one = (("y", "z"), ("y", "z"))
+    bufs_one = (ag1a, ag1b)
+    gather_own(
+        bufs_one, ((normed[:, 0:HALF], pos), (normed[:, HALF:D],)), order_one
     )
 
     pl.semaphore_wait(barrier, len(everyone))
 
-    first = gather_send((ag1a, ag1b), "y", "z", 0, 0)
-    for name in ("k", "v", "q", "out"):
+    state = gather_first(bufs_one, order_one, 0)
+    for name in ("k", "v", "up0", "up1"):
         send_weight(name)
     for slot, src, dst, axis in weights.values():
         copy = pltpu.make_async_copy(src, dst(place[axis]), local_sem.at[slot])
         copy.start()
         local.append(copy)
-    for copy in first:
-        copy.wait_recv()
-    second = gather_send((ag1a, ag1b), "y", "z", 0, 1)
-    send_weight("up")
-    send_weight("down")
+    gather_second(bufs_one, order_one, 0, state)
+    pass_weight("k")
+    pass_weight("v")
+    send_weight("q")
+    send_weight("out")
 
     lane_a = lax.broadcasted_iota(jnp.int32, (HC, HC), 0)
     lane_b = lax.broadcasted_iota(jnp.int32, (HC, HC), 1)
@@ -304,11 +336,12 @@
         lax.broadcasted_iota(jnp.int32, (PAD, HC), 0) == which, 1.0, 0.0
     ).astype(F32)
 
-    for name in ("k", "v", "q"):
-        pass_weight(name)
-    for copy in second:
-        copy.wait_recv()
-    gather_to_rows((ag1a, ag1b))
+    end_weight("k")
+    end_weight("v")
+    pass_weight("up0")
+    send_weight("down0")
+    pass_weight("q")
+    gather_end(bufs_one, order_one, "z", state)
     for z_at in range(SIDE):
         for y_at in range(SIDE):
             at = (z_at * SIDE + y_at) * ROWS
@@ -318,9 +351,7 @@
     sine = jnp.sin(angles)
     tokens = rows32[...].astype(BF)
 
-    pass_weight("out")
-    for name in ("k", "v", "q"):
-        end_weight(name)
+    pass_weight("up1")
 
     def heads(columns):
         values = columns.astype(BF).astype(F32)
@@ -347,6 +378,8 @@
         )
         for step in (1, 3, 2)
     ]
+    end_weight("q")
+    pass_weight("out")
     have_weight("q")
     queries = (heads(project(0)) * HD ** (-0.5)).astype(BF)
     for copy in moved:
@@ -367,7 +400,7 @@
     context = context[:, 64:256].astype(BF)
     have_weight("out")
 
-    def scatter_sum(send, recv, mid, last, produce, p, q, slot, meanwhile):
+    def scatter_sum(send, recv, mid, last, produce, p, q, slot, hooks):
         order = ((q, p), (p, q))
         copies = [[], []]
         for h in range(2):
@@ -388,7 +421,7 @@
                         dev(one, step),
                     )
                 )
-        meanwhile()
+        hooks[0]()
         second = [[], []]
         for h in range(2):
             one, two = order[h]
@@ -409,6 +442,7 @@
                         dev(two, step),
                     )
                 )
+        hooks[1]()
         halves = []
         for h in range(2):
             one, two = order[h]
@@ -429,28 +463,31 @@
         "y",
         "z",
         1,
-        lambda: pass_weight("up"),
+        (lambda: pass_weight("down0"), lambda: send_weight("down1")),
     )
     first_res = resid + modul(2) * attended
     normed_two = (layer_norm(first_res, 1e-05) * (1.0 + modul(4)) + modul(3)).astype(BF)
-    gather_start(
-        (ag2a, ag2b), ((normed_two[:, 0:HALF],), (normed_two[:, HALF:D],)), "x", "z"
-    )
-    for copy in gather_send((ag2a, ag2b), "x", "z", 2, 0):
-        copy.wait_recv()
-    second = gather_send((ag2a, ag2b), "x", "z", 2, 1)
-    pass_weight("down")
-    end_weight("up")
-    for copy in second:
-        copy.wait_recv()
-    gather_to_rows((ag2a, ag2b))
+    order_two = (("x", "z"), ("z", "x"))
+    bufs_two = (ag2a, ag2b)
+    gather_own(
+        bufs_two, ((normed_two[:, 0:HALF],), (normed_two[:, HALF:D],)), order_two
+    )
+    state = gather_first(bufs_two, order_two, 1)
+    gather_second(bufs_two, order_two, 1, state)
+    end_weight("up0")
+    end_weight("up1")
+    end_weight("down0")
+    pass_weight("down1")
+    gather_end(bufs_two, order_two, "z", state)
     tokens_two = rows32[...].astype(BF)
-    end_weight("down")
-    have_weight("up")
+    have_weight("up0")
+    have_weight("up1")
     inner = jax.nn.gelu(
         dot_nt(tokens_two, wup[...].reshape(SIDE * HID, D)), approximate=True
     ).astype(BF)
-    have_weight("down")
+    end_weight("down1")
+    have_weight("down0")
+    have_weight("down1")
     down_weight = wdown[...].reshape(SIDE * HID, D)
     reduced = scatter_sum(
         *rs2,
@@ -460,7 +497,7 @@
         "x",
         "z",
         3,
-        lambda: None,
+        (lambda: None, lambda: None),
     )
     near[2].wait()
     near[3].wait()
@@ -538,12 +575,14 @@
             sums(),
             sums(),
             pltpu.VMEM((SIDE * SIDE * ROWS, PAD), F32),
-            pltpu.SemaphoreType.DMA((6, 4, 2)),
-            pltpu.SemaphoreType.DMA((6, 4, 2)),
+            pltpu.SemaphoreType.DMA((8, 4, 2)),
+            pltpu.SemaphoreType.DMA((8, 4, 2)),
             pltpu.SemaphoreType.DMA((4,)),
-            pltpu.SemaphoreType.DMA((6,)),
+            pltpu.SemaphoreType.DMA((8,)),
             pltpu.SemaphoreType.DMA((5, 2, 2, 3)),
             pltpu.SemaphoreType.DMA((5, 2, 2, 3)),
+            pltpu.SemaphoreType.DMA((2, 2, 5, 3)),
+            pltpu.SemaphoreType.DMA((2, 2, 5, 3)),
         ],
         compiler_params=pltpu.CompilerParams(
             collective_id=0, has_side_effects=True, vmem_limit_bytes=56 << 20

time: 86.9 us -> 80.7 us (0.929)
  Pallas kernels: 84.2 us -> 77.9 us
    pallas_call x1, Pallas kernels: 84.2 us -> 77.9 us  [shards(): pl.pallas_call(kernel, out_shape=jax.ShapeDtypeStruct(latent.shape, F32),...]
where the time goes in v3:
time: 80.7 us; the launch traced here: 80.5 us
  Pallas kernels  77.9 us (97%)
  between operations  1.3 us (2%)
  local copies, waits for them, and re-layouts  1.28 us (2%)
    pallas_call x1, Pallas kernels, shards(): pl.pallas_call(kernel, out_shape=jax.ShapeDtypeStruct(latent.shape, F32),...  77.9 us

profile of v3, /device:TPU:1, one launch (start us, length us, event | category | flops | bytes accessed | tf_op | source)
XLA Modules:
  0.0 80.5 jit_solution(13095756773935456570)
XLA Ops:
  1.3 77.9 %step.1 = f32[8,32]{1,0:T(8,128)} custom-call(f32[8,32]{1,0:T(8,128)} %latent.1, s32[1,64]{1,0:T(1,128)} %bitcast.13, f32[1,192]{1,0:T(1,128)} %constant.2.clone.freq, s32[3,8]{1,0:T(4,128)} %bitcast.12, s32[64]{0:T(128)} %counts.1, s32[1]{0:T(128)S(6)} %copy.17.text_len, f32[1]{0:T(128)S(6)} %copy.18.guidance, f32[2]{0:T(128)} %solver.1, ...), custom_call_target="tpu_custom_call" | custom-call | tf_op jit(solution)/shard_map/step/pallas_call | solution.py:555
  79.2 1.3 %copy.19 = f32[8,32]{1,0:T(8,128)} copy(f32[8,32]{1,0:T(8,128)} %step.1) | data formatting | bytes 2048

commit v4 on v3

--- a/solution.py
+++ b/solution.py
@@ -49,16 +49,16 @@
 
 
 def kernel(
-    latent,
-    counts_row,
-    freq,
-    positions,
-    counts,
-    text_len,
-    guidance,
-    solver,
     hidden_far,
     modulation_far,
+    positions_far,
+    text_len_far,
+    counts_row_far,
+    counts_far,
+    freq_far,
+    latent_far,
+    guidance_far,
+    solver_far,
     out_mod_far,
     w_proj_far,
     w_qkv,
@@ -68,6 +68,14 @@
     out,
     hidden,
     modulation,
+    positions,
+    text_len,
+    counts_row,
+    counts,
+    freq,
+    latent,
+    guidance,
+    solver,
     out_mod,
     w_proj,
     wqkv,
@@ -131,6 +139,14 @@
         (
             (hidden_far, hidden),
             (modulation_far, modulation),
+            (positions_far, positions),
+            (text_len_far, text_len),
+            (counts_row_far, counts_row),
+            (counts_far, counts),
+            (freq_far, freq),
+            (latent_far, latent),
+            (guidance_far, guidance),
+            (solver_far, solver),
             (out_mod_far, out_mod),
             (w_proj_far, w_proj),
         )
@@ -218,8 +234,8 @@
             copy.wait_recv()
         local[weights[name][0]].wait()
 
-    near[0].wait()
-    near[1].wait()
+    for copy in near[:4]:
+        copy.wait()
     resid = hidden[...].astype(F32)
     row = lax.broadcasted_iota(jnp.int32, (ROWS, 1), 0)
     is_text = me * ROWS + row < text_len[0]
@@ -310,6 +326,8 @@
         copy.start()
         local.append(copy)
     gather_second(bufs_one, order_one, 0, state)
+    for copy in near[4:]:
+        copy.wait()
     pass_weight("k")
     pass_weight("v")
     send_weight("q")
@@ -499,8 +517,6 @@
         3,
         (lambda: None, lambda: None),
     )
-    near[2].wait()
-    near[3].wait()
     second_res = first_res + modul(5) * reduced
     final = (
         layer_norm(second_res, 1e-05) * (1.0 + out_mod[1:2, :]) + out_mod[0:1, :]
@@ -541,7 +557,6 @@
     solver,
 ):
     vmem = pl.BlockSpec(memory_space=pltpu.VMEM)
-    smem = pl.BlockSpec(memory_space=pltpu.SMEM)
     whole = pl.BlockSpec(memory_space=pl.ANY)
 
     def sums():
@@ -555,11 +570,19 @@
     return pl.pallas_call(
         kernel,
         out_shape=jax.ShapeDtypeStruct(latent.shape, F32),
-        in_specs=[vmem] * 3 + [smem] * 5 + [whole] * 8,
+        in_specs=[whole] * 16,
         out_specs=vmem,
         scratch_shapes=[
             pltpu.VMEM((ROWS, D), BF),
             pltpu.VMEM((6, 2, D), F32),
+            pltpu.SMEM((3, ROWS), jnp.int32),
+            pltpu.SMEM((1,), jnp.int32),
+            pltpu.VMEM((1, 64), jnp.int32),
+            pltpu.SMEM((64,), jnp.int32),
+            pltpu.VMEM((1, HC), F32),
+            pltpu.VMEM((ROWS, 32), F32),
+            pltpu.SMEM((1,), F32),
+            pltpu.SMEM((2,), F32),
             pltpu.VMEM((2, D), F32),
             pltpu.VMEM((64, D), BF),
             pltpu.VMEM((3, SIDE, 48, D), BF),
@@ -577,7 +600,7 @@
             pltpu.VMEM((SIDE * SIDE * ROWS, PAD), F32),
             pltpu.SemaphoreType.DMA((8, 4, 2)),
             pltpu.SemaphoreType.DMA((8, 4, 2)),
-            pltpu.SemaphoreType.DMA((4,)),
+            pltpu.SemaphoreType.DMA((12,)),
             pltpu.SemaphoreType.DMA((8,)),
             pltpu.SemaphoreType.DMA((5, 2, 2, 3)),
             pltpu.SemaphoreType.DMA((5, 2, 2, 3)),
@@ -589,16 +612,16 @@
         ),
         name="step",
     )(
+        hidden[0],
+        modulation.transpose(1, 0, 2),
+        positions.T,
+        text_len,
+        counts[None, :],
+        counts,
+        jnp.asarray(frequencies()),
         latent,
-        counts[None, :],
-        jnp.asarray(frequencies()),
-        positions.T,
-        counts,
-        text_len,
         guidance,
         solver,
-        hidden[0],
-        modulation.transpose(1, 0, 2),
         out_mod,
         w_proj.T,
         w_qkv.transpose(1, 2, 0),

time: 80.7 us -> 79.9 us (0.990)
  no operation moved by 1% of the time
where the time goes in v4:
time: 79.9 us; the launch traced here: 79.7 us
  Pallas kernels  77.1 us (96%)
  between operations  1.3 us (2%)
  local copies, waits for them, and re-layouts  1.28 us (2%)
    pallas_call x1, Pallas kernels, shards(): pl.pallas_call(kernel, out_shape=jax.ShapeDtypeStruct(latent.shape, F32),...  77.1 us

profile of v4, /device:TPU:1, one launch (start us, length us, event | category | flops | bytes accessed | tf_op | source)
XLA Modules:
  0.0 79.7 jit_solution(10185061874928595039)
XLA Ops:
  1.3 77.1 %step.1 = f32[8,32]{1,0:T(8,128)} custom-call(bf16[8,3072]{1,0:T(8,128)(2,1)} %bitcast.11, f32[6,2,3072]{2,1,0:T(2,128)} %bitcast.10, s32[3,8]{1,0:T(4,128)} %bitcast.12, s32[1]{0:T(128)S(6)} %copy.17.text_len_far, s32[1,64]{1,0:T(1,128)} %bitcast.13, s32[64]{0:T(128)} %counts_far.1, f32[1,192]{1,0:T(1,128)} %constant.2.clone.freq_far, f32[8,32]{1,0:T(8,128)} %latent_far.1, ...), custom_call_target="tpu_custom_call" | custom-call | tf_op jit(solution)/shard_map/step/pallas_call | solution.py:570
  78.4 1.3 %copy.19 = f32[8,32]{1,0:T(8,128)} copy(f32[8,32]{1,0:T(8,128)} %step.1) | data formatting | bytes 2048

commit v5 on v4

--- a/solution.py
+++ b/solution.py
@@ -281,7 +281,7 @@
                 g_recv.at[slot, h, behind + 1, step - 1],
                 dev(q, step),
             )
-            for step in (1, 3, 2)
+            for step in (2, 1, 3)
         ]
 
     def gather_second(bufs, orders, slot, state):
@@ -358,7 +358,6 @@
     end_weight("v")
     pass_weight("up0")
     send_weight("down0")
-    pass_weight("q")
     gather_end(bufs_one, order_one, "z", state)
     for z_at in range(SIDE):
         for y_at in range(SIDE):
@@ -369,8 +368,6 @@
     sine = jnp.sin(angles)
     tokens = rows32[...].astype(BF)
 
-    pass_weight("up1")
-
     def heads(columns):
         values = columns.astype(BF).astype(F32)
         center = values - exact_dot(values, average)
@@ -381,6 +378,7 @@
     def project(part):
         return dot_nt(tokens, wqkv[part].reshape(HC, D))
 
+    pass_weight("q")
     have_weight("k")
     keys = heads(project(1)).astype(BF)
     have_weight("v")
@@ -394,10 +392,11 @@
             c_recv.at[4, 0, 0, step - 1],
             dev("x", step),
         )
-        for step in (1, 3, 2)
+        for step in (2, 1, 3)
     ]
     end_weight("q")
     pass_weight("out")
+    pass_weight("up1")
     have_weight("q")
     queries = (heads(project(0)) * HD ** (-0.5)).astype(BF)
     for copy in moved:
@@ -428,7 +427,7 @@
                     at = (q_at * SIDE + p_at) * ROWS
                     i, j = (q_at, p_at) if h == 0 else (p_at, q_at)
                     send[h, i, j] = part[at : at + ROWS, :].astype(BF)
-            for step in (1, 3, 2):
+            for step in (2, 1, 3):
                 one = order[h][0]
                 copies[h].append(
                     remote(
@@ -450,7 +449,7 @@
                 for k in range(3):
                     total = total + recv[h, k, j].astype(F32)
                 mid[h, j] = total.astype(BF)
-            for step in (1, 3, 2):
+            for step in (2, 1, 3):
                 second[h].append(
                     remote(
                         mid.at[h, (place[two] + step) % 4],

time: 79.9 us -> 78.9 us (0.987)
  Pallas kernels: 77.1 us -> 76.2 us
    pallas_call x1, Pallas kernels: 77.1 us -> 76.2 us  [shards(): pl.pallas_call(kernel, out_shape=jax.ShapeDtypeStruct(latent.shape, F32),...]
where the time goes in v5:
time: 78.9 us; the launch traced here: 78.7 us
  Pallas kernels  76.2 us (97%)
  between operations  1.3 us (2%)
  local copies, waits for them, and re-layouts  1.28 us (2%)
    pallas_call x1, Pallas kernels, shards(): pl.pallas_call(kernel, out_shape=jax.ShapeDtypeStruct(latent.shape, F32),...  76.2 us

profile of v5, /device:TPU:1, one launch (start us, length us, event | category | flops | bytes accessed | tf_op | source)
XLA Modules:
  0.0 78.7 jit_solution(8799794966862148589)
XLA Ops:
  1.3 76.2 %step.1 = f32[8,32]{1,0:T(8,128)} custom-call(bf16[8,3072]{1,0:T(8,128)(2,1)} %bitcast.11, f32[6,2,3072]{2,1,0:T(2,128)} %bitcast.10, s32[3,8]{1,0:T(4,128)} %bitcast.12, s32[1]{0:T(128)S(6)} %copy.17.text_len_far, s32[1,64]{1,0:T(1,128)} %bitcast.13, s32[64]{0:T(128)} %counts_far.1, f32[1,192]{1,0:T(1,128)} %constant.2.clone.freq_far, f32[8,32]{1,0:T(8,128)} %latent_far.1, ...), custom_call_target="tpu_custom_call" | custom-call | tf_op jit(solution)/shard_map/step/pallas_call | solution.py:569
  77.5 1.3 %copy.19 = f32[8,32]{1,0:T(8,128)} copy(f32[8,32]{1,0:T(8,128)} %step.1) | data formatting | bytes 2048

commit v6 on v5

--- a/solution.py
+++ b/solution.py
@@ -265,9 +265,10 @@
                         g_recv.at[slot, h, 0, step - 1],
                         dev(p, step),
                     )
-                    for step in (1, 3, 2)
+                    for step in (2, 1, 3)
                 ]
             )
+        first = [[right, left, far] for far, right, left in first]
         return first, [gather_pass(bufs[h], orders[h], slot, h, 0) for h in range(2)]
 
     def gather_pass(buf, order, slot, h, behind):

time: 78.9 us -> 78.9 us (level)
  no operation moved by 1% of the time
where the time goes in v6:
time: 78.9 us; the launch traced here: 78.7 us
  Pallas kernels  76.2 us (97%)
  between operations  1.3 us (2%)
  local copies, waits for them, and re-layouts  1.28 us (2%)
    pallas_call x1, Pallas kernels, shards(): pl.pallas_call(kernel, out_shape=jax.ShapeDtypeStruct(latent.shape, F32),...  76.2 us

profile of v6, /device:TPU:1, one launch (start us, length us, event | category | flops | bytes accessed | tf_op | source)
XLA Modules:
  0.0 78.7 jit_solution(3847011072588410014)
XLA Ops:
  1.3 76.2 %step.1 = f32[8,32]{1,0:T(8,128)} custom-call(bf16[8,3072]{1,0:T(8,128)(2,1)} %bitcast.11, f32[6,2,3072]{2,1,0:T(2,128)} %bitcast.10, s32[3,8]{1,0:T(4,128)} %bitcast.12, s32[1]{0:T(128)S(6)} %copy.17.text_len_far, s32[1,64]{1,0:T(1,128)} %bitcast.13, s32[64]{0:T(128)} %counts_far.1, f32[1,192]{1,0:T(1,128)} %constant.2.clone.freq_far, f32[8,32]{1,0:T(8,128)} %latent_far.1, ...), custom_call_target="tpu_custom_call" | custom-call | tf_op jit(solution)/shard_map/step/pallas_call | solution.py:570
  77.5 1.3 %copy.19 = f32[8,32]{1,0:T(8,128)} copy(f32[8,32]{1,0:T(8,128)} %step.1) | data formatting | bytes 2048
